TPU v7x, 512 devices: a whole 4x4x16 slice. The times are simulated.
512 devices in a mesh: section: 32 (over y, x, core), ctx: 16 (over z).
Axes of the slice: x: 4, y: 4, z: 16, core: 2. Of those that a mesh axis runs over, the one named last changes fastest.
Arguments:
- streams: bfloat16 [32, 2048, 5120], P('section', 'ctx'), may hold values from -6 to 6
- conv_weight: bfloat16 [32, 4, 5120], P('section'), may hold values from -3 to 3
- beta_logit: float32 [32, 2048, 16], P('section', 'ctx'), may hold values from -12 to 3
- gate_log: float32 [32, 2048, 8], P('section', 'ctx'), may hold values from -2 to 0
- norm_gain: float32 [32, 1024], P('section'), may hold values from 0.25 to 1.75
- w_out: bfloat16 [32, 1024, 2048], P('section', None, 'ctx'), may hold values from -0.1875 to 0.1875
Outputs:
- handed: bfloat16 [32, 2048, 2048], P('section', 'ctx')
All inputs are finite; a program needn't handle non-finite values.
Results may differ from a plain program's by a relative error of at most 0.0049.
Values may be sent and summed in bfloat16 or wider, within the bound.
A program may use at most 128 MiB of HBM per device.

v0:
```python
import jax
import jax.numpy as jnp
from jax import lax
from jax.sharding import PartitionSpec as P

HEAD_TOTAL = 8
HK = 128
STEPS = 2
CONV = 4
SPAN = 128
highest = lax.Precision.HIGHEST


def shifted(value, axis, steps):
    count = lax.axis_size(axis)
    first, last = (max(0, -steps), min(count, count - steps))
    return lax.ppermute(value, axis, [(source, source + steps) for source in range(first, last)])


def entering(value, axis, join, neutral):
    count, mine = (lax.axis_size(axis), lax.axis_index(axis))
    pieces = jax.tree.map(lambda part: lax.all_gather(part, axis), value)
    total = jax.tree.map(
        lambda part, zero: jnp.full_like(part, 0) + jnp.asarray(zero, part.dtype), value, neutral
    )

    def turn(position, total):
        longer = join(total, jax.tree.map(lambda part: part[position], pieces))
        return jax.tree.map(lambda new, old: jnp.where(position < mine, new, old), longer, total)

    return lax.fori_loop(0, count - 1, turn, total)


def passed_along(value, axis, steps):
    count = lax.axis_size(axis)
    pairs = [(source, (source + steps) % count) for source in range(count)]
    return lax.ppermute(value, axis, pairs)


def mix_taps(extended, tap_weights):
    tok_count = extended.shape[0] - tap_weights.shape[0] + 1
    summed = jnp.zeros((tok_count, extended.shape[1]), jnp.float32)
    for offset in range(tap_weights.shape[0]):
        summed = summed + tap_weights[offset].astype(jnp.float32) * extended[
            offset : offset + tok_count
        ].astype(jnp.float32)
    return jax.nn.silu(summed)


def unit_rows(vectors):
    return vectors * lax.rsqrt(jnp.sum(vectors * vectors, axis=-1, keepdims=True) + 1e-06)


def head_major(active, beta_logit, gate_log):
    tok_count = active.shape[0]
    head_width = HEAD_TOTAL * HK
    queries = unit_rows(active[:, :head_width].reshape(tok_count, HEAD_TOTAL, HK)).transpose(
        1, 0, 2
    )
    keys_all = unit_rows(
        active[:, head_width : (1 + STEPS) * head_width].reshape(tok_count, STEPS, HEAD_TOTAL, HK)
    )
    keys_all = keys_all.transpose(2, 0, 1, 3).reshape(HEAD_TOTAL, tok_count * STEPS, HK)
    values_all = active[:, (1 + STEPS) * head_width :].reshape(tok_count, STEPS, HEAD_TOTAL, HK)
    values_all = values_all.transpose(2, 0, 1, 3).reshape(HEAD_TOTAL, tok_count * STEPS, HK)
    step_size = (
        jax.nn.sigmoid(beta_logit.reshape(tok_count, STEPS, HEAD_TOTAL))
        .transpose(2, 0, 1)
        .reshape(HEAD_TOTAL, tok_count * STEPS)
    )
    opening = (lax.broadcasted_iota(jnp.int32, (1, STEPS, 1), 1) == 0).astype(gate_log.dtype)
    log_gate = (
        (gate_log[:, None, :] * opening).transpose(2, 0, 1).reshape(HEAD_TOTAL, tok_count * STEPS)
    )
    return (queries, keys_all, values_all, step_size, log_gate)


def span_terms(queries, keys_all, values_all, step_size, log_gate):
    head_count, virtual, head_dim = keys_all.shape
    blocks = virtual // SPAN
    per_block = SPAN // STEPS
    queries = queries.reshape(head_count, blocks, per_block, head_dim)
    keys_all = keys_all.reshape(head_count, blocks, SPAN, head_dim)
    values_all = values_all.reshape(head_count, blocks, SPAN, head_dim)
    step_size = step_size.reshape(head_count, blocks, SPAN)
    cumulate = jnp.cumsum(log_gate.reshape(head_count, blocks, SPAN), axis=-1)
    query_log = cumulate[..., STEPS - 1 :: STEPS]
    row_index = lax.broadcasted_iota(jnp.int32, (SPAN, SPAN), 0)
    col_index = lax.broadcasted_iota(jnp.int32, (SPAN, SPAN), 1)
    strict = col_index < row_index
    spread = cumulate[..., :, None] - cumulate[..., None, :]
    damping = jnp.where(strict, jnp.exp(jnp.where(strict, spread, 0.0)), 0.0)
    key_inner = jnp.einsum("hcid,hcjd->hcij", keys_all, keys_all, precision=highest)
    unit_lower = (
        jnp.eye(SPAN, dtype=key_inner.dtype) + step_size[..., :, None] * damping * key_inner
    )
    right_sides = jnp.concatenate(
        [step_size[..., None] * values_all, (step_size * jnp.exp(cumulate))[..., None] * keys_all],
        axis=-1,
    )
    solved = jax.scipy.linalg.solve_triangular(
        unit_lower, right_sides, lower=True, unit_diagonal=True
    )
    value_part = solved[..., :head_dim]
    key_part = solved[..., head_dim:]
    to_end = keys_all * jnp.exp(cumulate[..., -1:] - cumulate)[..., None]
    carried = jnp.exp(cumulate[..., -1])[..., None, None] * jnp.eye(head_dim, dtype=key_inner.dtype)
    carried = carried - jnp.einsum("hcid,hcie->hcde", to_end, key_part, precision=highest)
    written = jnp.einsum("hcid,hcie->hcde", to_end, value_part, precision=highest)
    query_row = lax.broadcasted_iota(jnp.int32, (per_block, SPAN), 0) * STEPS + STEPS - 1
    query_col = lax.broadcasted_iota(jnp.int32, (per_block, SPAN), 1)
    allowed = query_col <= query_row
    query_spread = query_log[..., :, None] - cumulate[..., None, :]
    query_damping = jnp.where(allowed, jnp.exp(jnp.where(allowed, query_spread, 0.0)), 0.0)
    scores = jnp.einsum("hcpd,hcid->hcpi", queries, keys_all, precision=highest) * query_damping
    direct = jnp.einsum("hcpi,hcie->hcpe", scores, value_part, precision=highest)
    reach_map = queries * jnp.exp(query_log)[..., None] - jnp.einsum(
        "hcpi,hcie->hcpe", scores, key_part, precision=highest
    )
    return (
        jnp.moveaxis(carried, 1, 0),
        jnp.moveaxis(written, 1, 0),
        jnp.moveaxis(direct, 1, 0),
        jnp.moveaxis(reach_map, 1, 0),
    )


def advance(state_now, piece_terms):
    carried, written, direct, reach_map = piece_terms
    span_out = direct + jnp.einsum("hpd,hde->hpe", reach_map, state_now, precision=highest)
    state_now = jnp.einsum("hde,hef->hdf", carried, state_now, precision=highest) + written
    return (state_now, span_out)


def normalize(outputs, norm_gain):
    tok_count = outputs.shape[0]
    inverse_rms = lax.rsqrt(jnp.mean(outputs * outputs, axis=-1, keepdims=True) + 1e-05)
    return (
        (outputs * inverse_rms * norm_gain.reshape(HEAD_TOTAL, HK))
        .reshape(tok_count, HEAD_TOTAL * HK)
        .astype(jnp.bfloat16)
    )


def combine_pairs(earlier_pair, later_pair):
    first_map, first_add = earlier_pair
    second_map, second_add = later_pair
    joined_map = jnp.einsum("hde,hef->hdf", second_map, first_map, precision=highest)
    joined_add = jnp.einsum("hde,hef->hdf", second_map, first_add, precision=highest) + second_add
    return (joined_map, joined_add)


def compose_step(carried_in, piece_terms):
    so_far, added_state = carried_in
    next_map = jnp.einsum("hde,hef->hdf", piece_terms[0], so_far, precision=highest)
    next_add = (
        jnp.einsum("hde,hef->hdf", piece_terms[0], added_state, precision=highest) + piece_terms[1]
    )
    return ((next_map, next_add), None)


def on_device(streams, conv_weight, beta_logit, gate_log, norm_gain, w_out):
    own_rows = streams[0]
    tok_count = own_rows.shape[0]
    rim_rows = shifted(own_rows[tok_count - (CONV - 1) :], "ctx", 1)
    active = mix_taps(jnp.concatenate([rim_rows, own_rows], axis=0), conv_weight[0])
    span_parts = span_terms(*head_major(active, beta_logit[0], gate_log[0]))
    identity_map = jnp.broadcast_to(jnp.eye(HK, dtype=jnp.float32), (HEAD_TOTAL, HK, HK))
    nothing = jnp.zeros((HEAD_TOTAL, HK, HK), jnp.float32)
    (total_map, total_add), _ = lax.scan(compose_step, (identity_map, nothing), span_parts)
    _, incoming = entering((total_map, total_add), "ctx", combine_pairs, (identity_map, nothing))
    _, outputs = lax.scan(advance, incoming, span_parts)
    outputs = outputs.transpose(0, 2, 1, 3).reshape(tok_count, HEAD_TOTAL, HK)
    normed = normalize(outputs, norm_gain[0])
    local_cols = w_out[0]
    mixed_rows = jnp.dot(
        normed,
        lax.all_gather(local_cols, "ctx", axis=1, tiled=True),
        preferred_element_type=jnp.float32,
    ).astype(jnp.bfloat16)
    return passed_along(mixed_rows[None], "section", 1)


def solution(mesh):
    placed = (
        P("section", "ctx", None),
        P("section", None, None),
        P("section", "ctx", None),
        P("section", "ctx", None),
        P("section", None),
        P("section", None, "ctx"),
    )
    return jax.shard_map(
        on_device, mesh=mesh, in_specs=placed, out_specs=P("section", "ctx", None), check_vma=False
    )
```

profile of v0, /device:TPU:32, one launch (start us, length us, event | category | flops | bytes accessed | tf_op | source)
XLA Modules:
  0.0 527.9 jit_solution(1281271470755481892)
XLA Ops:
  7.6 3.8 collective-permute-start
  22.7 2.4 fusion.43
  25.1 157.9 %custom-call.4 = f32[8,2,1,128,128]{3,4,2,1,0:T(8,128)} custom-call(f32[8,2,1,128,128]{4,3,2,1,0:T(8,128)S(1)} %fusion.43), custom_call_target="InvertDiagBlocksLowerTriangular" | custom-call | tf_op jit(solution)/shard_map/jit(_solve_triangular)/vmap(vmap())/triangular_solve | solution.py:101
  183.0 1.9 broadcast_multiply_fusion
  184.9 2.0 fusion.35
  186.9 2.2 convolution_bitcast_fusion
  189.3 2.2 fusion.39
  191.7 2.9 while.40
  199.0 2.1 convolution_multiply_fusion.1
  204.1 97.6 %all-gather.7.cloned.1.call-done = f32[128,128,128]{2,1,0:T(8,128)} async-done(((f32[8,128,128]{2,1,0:T(8,128)}), f32[128,128,128]{2,1,0:T(8,128)}) %all-gather.7.cloned.1.call-update) | async-done | bytes 8388624 | tf_op jit(solution)/shard_map/all_gather | solution.py:22
  301.7 105.9 %all-gather.9.cloned.1.call-done = f32[128,128,128]{2,1,0:T(8,128)} async-done(((f32[8,128,128]{2,1,0:T(8,128)}), f32[128,128,128]{2,1,0:T(8,128)}) %all-gather.9.cloned.1.call-update) | async-done | bytes 8388624 | tf_op jit(solution)/shard_map/all_gather | solution.py:22
  407.6 29.2 %while.41 = (s32[]{:T(128)}, f32[8,128,128]{2,1,0:T(8,128)S(1)}, s32[]{:T(128)}, f32[16,8,128,128]{3,2,1,0:T(8,128)}, f32[16,8,128,128]{3,2,1,0:T(8,128)}, /*index=5*/s32[]{:T(128)}, s32[]{:T(128)}) while((s32[]{:T(128)}, f32[8,128,128]{2,1,0:T(8,128)S(1)}, s32[]{:T(128)}, f32[16,8,128,128]{3,2,1,0:T(8,128)}, ...), condition=%wide.region_5.6_spmd.clone, body=%wide.region_4.5_spmd.clone.sunk | while | flops 201850880 | bytes 3672671 | solution.py:31
  407.6 1.9 fusion.97
  409.6 1.9 fusion.97
  413.5 1.9 fusion.97
  415.4 1.9 fusion.97
  417.4 1.9 fusion.97
  419.3 1.9 fusion.97
  421.3 1.9 fusion.97
  423.2 1.9 fusion.97
  425.2 1.9 fusion.97
  427.1 1.9 fusion.97
  429.1 1.9 fusion.97
  431.0 1.9 fusion.97
  434.9 1.9 fusion.97
  436.8 6.0 %while.39 = (s32[]{:T(128)}, f32[8,128,128]{2,1,0:T(8,128)S(1)}, f32[2,8,64,128]{3,2,1,0:T(8,128)}, f32[2,8,128,128]{3,2,1,0:T(8,128)S(1)}, f32[2,8,128,128]{3,2...) while((s32[]{:T(128)}, f32[8,128,128]{2,1,0:T(8,128)S(1)}, ...), condition=%wide.region_8.9_spmd, body=%wide.region_7.8_spmd.sunk | while | flops 302186496 | bytes 4458581 | solution.py:172
  436.9 2.3 fusion.89
  439.9 2.3 fusion.89
  445.5 58.0 %all-gather.11.cloned.1.call-done = bf16[1,1024,2048]{2,1,0:T(8,128)(2,1)} async-done(((bf16[1,1024,128]{2,1,0:T(8,128)(2,1)}), bf16[1,1024,2048]{2,1,0:T(8,128)(2,1)}) %all-gather.11.cloned.1.call-update) | async-done | bytes 4194320 | tf_op jit(solution)/shard_map/all_gather | solution.py:178
  503.7 3.0 fusion.32
  506.7 1.9 collective-permute-start.1
  508.7 11.9 %collective-permute-done.1 = bf16[1,128,2048]{2,1,0:T(8,128)(2,1)S(1)} collective-permute-done((bf16[1,128,2048]{2,1,0:T(8,128)(2,1)S(1)}, bf16[1,128,2048]{2,1,0:T(8,128)(2,1)S(1)}, u32[]{:S(2)}, u32[]{:S(2)}) %collective-permute-start.1) | collective-permute-done | bytes 524320 | tf_op jit(solution)/shard_map/ppermute | solution.py:37
  (115 shorter events, 31.8 us)
Async XLA Ops:
  6.5 9.7 %copy-start.7 = (bf16[1,128,5120]{2,1,0:T(8,128)(2,1)S(1)}, bf16[1,128,5120]{2,1,0:T(8,128)(2,1)}, u32[]{:S(2)}) copy-start(bf16[1,128,5120]{2,1,0:T(8,128)(2,1)} %param.12) | copy-start | bytes 3932164
  6.5 295.1 %all-gather.7.cloned.1.call-start = ((), (), s32[]{:S(2)}) async-start(), calls=%async_computation | async-start | bytes 8912896 | tf_op jit(solution)/shard_map/all_gather | solution.py:22
  7.6 8.7 %collective-permute-start = (bf16[3,5120]{1,0:T(4,128)(2,1)S(1)}, bf16[3,5120]{1,0:T(4,128)(2,1)S(1)}, u32[]{:S(2)}, u32[]{:S(2)}) collective-permute-start(bf16[3,5120]{1,0:T(4,128)(2,1)S(1)} %slice_bitcast_fusion.3), channel_id=1, source_target_pairs={{0,1},{1,2},{2,3},{3,4},{4,5},{5,6},{6,7},{7,8},{8,9},{9,10},{10,1... | collective-permute-start | bytes 92168 | tf_op jit(solution)/shard_map/ppermute | solution.py:17
  18.1 1.5 copy-start.6
  21.0 168.3 %copy-start = (f32[8,128,2,128]{3,2,1,0:T(2,128)}, f32[8,128,2,128]{3,2,1,0:T(2,128)S(1)}, u32[]{:S(2)}) copy-start(f32[8,128,2,128]{3,2,1,0:T(2,128)S(1)} %copy.83) | copy-start | bytes 3145732
  183.0 1.9 copy-start.8
  186.9 2.3 copy-start.3
  194.5 0.8 copy-start.2
  194.5 1.0 copy-start.5
  195.4 212.2 %all-gather.9.cloned.1.call-start = ((), (), s32[]{:S(2)}) async-start(), calls=%async_computation.1 | async-start | bytes 8912896 | tf_op jit(solution)/shard_map/all_gather | solution.py:22
  196.1 307.4 %all-gather.11.cloned.1.call-start = ((), (), s32[]{:S(2)}) async-start(), calls=%async_computation.2 | async-start | bytes 4456448 | tf_op jit(solution)/shard_map/all_gather | solution.py:178
  197.1 1.9 copy-start.1
  198.5 2.7 copy-start.4
  436.8 66.9 %copy-start.9 = (f32[1,1024]{1,0:T(1,128)S(1)}, f32[1,1024]{1,0:T(1,128)}, u32[]{:S(2)}) copy-start(f32[1,1024]{1,0:T(1,128)} %param.16) | copy-start | bytes 12292
  506.7 13.8 %collective-permute-start.1 = (bf16[1,128,2048]{2,1,0:T(8,128)(2,1)S(1)}, bf16[1,128,2048]{2,1,0:T(8,128)(2,1)S(1)}, u32[]{:S(2)}, u32[]{:S(2)}) collective-permute-start(bf16[1,128,2048]{2,1,0:T(8,128)(2,1)S(1)} %fusion.32), channel_id=1, source_target_pairs={{0,16},{16,32},{32,48},{48,64},{64,80},{80,96},{96,112},{112,128},... | collective-permute-start | bytes 1572872 | tf_op jit(solution)/shard_map/ppermute | solution.py:37
Sparse Core Ops, SparseCore 0:
  195.5 106.1 all-gather.6
  303.8 103.7 all-gather.8
  409.6 93.8 all-gather.10
where the time goes:
time: 529 us; the launch traced here: 528 us
  waiting for transfers between devices  275 us (52%)
  other arithmetic  167 us (32%)
  matrix products  53.5 us (10%)
  between operations  13.6 us (3%)
  local copies, waits for them, and re-layouts  12.2 us (2%)
  starting transfers between devices  6.05 us (1%)
    all_gather x2, waiting for transfers between devices, entering(): pieces = jax.tree.map(lambda part: lax.all_gather(part, axis), value)  203 us
    another operation x2, other arithmetic, span_terms(): jax.scipy.linalg.solve_triangular(unit_lower, right_sides, lower=True, un...  158 us
    all_gather x1, waiting for transfers between devices, on_device(): lax.all_gather(local_cols, 'ctx', axis=1, tiled=True)  58 us
    dot_general x15, matrix products, combine_pairs(): jnp.einsum('hde,hef->hdf', second_map, first_add, precision=highest)  28.1 us
    ppermute x1, waiting for transfers between devices, passed_along(): return lax.ppermute(value, axis, pairs)  11.9 us
  transfers between devices with their start and end apart: 5, of which 5 were waited for; matrix products, arithmetic and copies ran while one was open for 9% of the time, Pallas kernels for 0%

commit v1 on v0

--- a/solution.py
+++ b/solution.py
@@ -9,6 +9,14 @@
 CONV = 4
 SPAN = 128
 highest = lax.Precision.HIGHEST
+
+
+def tiled_gather(value, axis, dim):
+    devices = lax.axis_size(axis)
+    repeats = [devices if d == dim else 1 for d in range(value.ndim)]
+    return lax.all_to_all(
+        jnp.tile(value, repeats), axis, split_axis=dim, concat_axis=dim, tiled=True
+    )
 
 
 def shifted(value, axis, steps):
@@ -174,9 +182,7 @@
     normed = normalize(outputs, norm_gain[0])
     local_cols = w_out[0]
     mixed_rows = jnp.dot(
-        normed,
-        lax.all_gather(local_cols, "ctx", axis=1, tiled=True),
-        preferred_element_type=jnp.float32,
+        normed, tiled_gather(local_cols, "ctx", 1), preferred_element_type=jnp.float32
     ).astype(jnp.bfloat16)
     return passed_along(mixed_rows[None], "section", 1)
 

time: 529 us -> 650 us (1.23)
  the two profiles are of different devices: /device:TPU:32 before, /device:TPU:8 now
where the time goes in v1:
time: 650 us; the launch traced here: 648 us
  waiting for transfers between devices  371 us (57%)
  other arithmetic  168 us (26%)
  matrix products  54.2 us (8%)
  starting transfers between devices  20.4 us (3%)
  local copies, waits for them, and re-layouts  19.8 us (3%)
  between operations  13.9 us (2%)
    all_to_all x1, waiting for transfers between devices, tiled_gather(): lax.all_to_all(jnp.tile(value, repeats), axis, split_axis=dim, concat_axi...  221 us
    another operation x2, other arithmetic, span_terms(): jax.scipy.linalg.solve_triangular(unit_lower, right_sides, lower=True, un...  158 us
    all_gather x2, waiting for transfers between devices, entering(): pieces = jax.tree.map(lambda part: lax.all_gather(part, axis), value)  139 us
    dot_general x15, matrix products, combine_pairs(): jnp.einsum('hde,hef->hdf', second_map, first_add, precision=highest)  28.1 us
    all_to_all x1, starting transfers between devices, tiled_gather(): lax.all_to_all(jnp.tile(value, repeats), axis, split_axis=dim, concat_axi...  14.4 us
  transfers between devices with their start and end apart: 5, of which 4 were waited for; matrix products, arithmetic and copies ran while one was open for 3% of the time, Pallas kernels for 0%

profile of v1, /device:TPU:8, one launch (start us, length us, event | category | flops | bytes accessed | tf_op | source)
XLA Modules:
  0.0 648.5 jit_solution(3131241090048343996)
XLA Ops:
  7.6 3.8 collective-permute-start
  22.1 2.4 fusion.36
  24.5 157.9 %custom-call.4 = f32[8,2,1,128,128]{3,4,2,1,0:T(8,128)} custom-call(f32[8,2,1,128,128]{4,3,2,1,0:T(8,128)S(1)} %fusion.36), custom_call_target="InvertDiagBlocksLowerTriangular" | custom-call | tf_op jit(solution)/shard_map/jit(_solve_triangular)/vmap(vmap())/triangular_solve | solution.py:109
  182.4 1.9 broadcast_multiply_fusion
  184.3 2.0 fusion.28
  186.3 2.2 convolution_bitcast_fusion
  188.7 2.2 fusion.32
  191.1 2.9 while.40
  194.8 2.8 tile.9
  197.5 14.4 %all-to-all-start = ((bf16[1024,16,128]{2,0,1:T(8,128)(2,1)}), bf16[1024,16,128]{2,0,1:T(8,128)(2,1)}, u32[]{:S(2)}, u32[]{:S(2)}) async-start(bf16[1024,16,128]{2,0,1:T(8,128)(2,1)} %tile.9), calls=%async_computation | async-start | bytes 8388608 | tf_op jit(solution)/shard_map/all_to_all | solution.py:17
  214.8 2.1 convolution_multiply_fusion.1
  217.0 1.9 convolution_bitcast_fusion.2
  219.9 220.9 %all-to-all-done = bf16[1024,16,128]{2,0,1:T(8,128)(2,1)} async-done(((bf16[1024,16,128]{2,0,1:T(8,128)(2,1)}), bf16[1024,16,128]{2,0,1:T(8,128)(2,1)}, u32[]{:S(2)}, u32[]{:S(2)}) %all-to-all-start) | async-done | bytes 4194336 | tf_op jit(solution)/shard_map/all_to_all | solution.py:17
  440.8 6.4 copy.106
  447.3 32.8 %all-gather.5.cloned.1.call-done = f32[128,128,128]{2,1,0:T(8,128)} async-done(((f32[8,128,128]{2,1,0:T(8,128)}), f32[128,128,128]{2,1,0:T(8,128)}) %all-gather.5.cloned.1.call-update) | async-done | bytes 8388624 | tf_op jit(solution)/shard_map/all_gather | solution.py:30
  480.0 106.6 %all-gather.7.cloned.1.call-done = f32[128,128,128]{2,1,0:T(8,128)} async-done(((f32[8,128,128]{2,1,0:T(8,128)}), f32[128,128,128]{2,1,0:T(8,128)}) %all-gather.7.cloned.1.call-update) | async-done | bytes 8388624 | tf_op jit(solution)/shard_map/all_gather | solution.py:30
  586.6 29.2 %while.41 = (s32[]{:T(128)}, f32[8,128,128]{2,1,0:T(8,128)S(1)}, s32[]{:T(128)}, f32[16,8,128,128]{3,2,1,0:T(8,128)}, f32[16,8,128,128]{3,2,1,0:T(8,128)}, /*index=5*/s32[]{:T(128)}, s32[]{:T(128)}) while((s32[]{:T(128)}, f32[8,128,128]{2,1,0:T(8,128)S(1)}, s32[]{:T(128)}, f32[16,8,128,128]{3,2,1,0:T(8,128)}, ...), condition=%wide.region_5.6_spmd.clone, body=%wide.region_4.5_spmd.clone.sunk | while | flops 201850880 | bytes 3672671 | solution.py:39
  586.7 1.9 fusion.92
  588.6 1.9 fusion.92
  590.6 1.9 fusion.92
  592.5 1.9 fusion.92
  596.4 1.9 fusion.92
  598.3 1.9 fusion.92
  600.3 1.9 fusion.92
  602.2 1.9 fusion.92
  604.2 1.9 fusion.92
  615.8 5.9 while.39
  615.9 2.3 fusion.84
  618.9 2.3 fusion.84
  624.5 3.7 fusion.27
  628.2 1.9 collective-permute-start.1
  630.1 10.7 %collective-permute-done.1 = bf16[1,128,2048]{2,1,0:T(8,128)(2,1)S(1)} collective-permute-done((bf16[1,128,2048]{2,1,0:T(8,128)(2,1)S(1)}, bf16[1,128,2048]{2,1,0:T(8,128)(2,1)S(1)}, u32[]{:S(2)}, u32[]{:S(2)}) %collective-permute-start.1) | collective-permute-done | bytes 524320 | tf_op jit(solution)/shard_map/ppermute | solution.py:45
  (117 shorter events, 35.8 us)
Async XLA Ops:
  6.5 9.1 %copy-start.7 = (bf16[1,128,5120]{2,1,0:T(8,128)(2,1)S(1)}, bf16[1,128,5120]{2,1,0:T(8,128)(2,1)}, u32[]{:S(2)}) copy-start(bf16[1,128,5120]{2,1,0:T(8,128)(2,1)} %param.12) | copy-start | bytes 3932164
  6.5 473.5 %all-gather.5.cloned.1.call-start = ((), (), s32[]{:S(2)}) async-start(), calls=%async_computation.1 | async-start | bytes 8912896 | tf_op jit(solution)/shard_map/all_gather | solution.py:30
  7.6 8.1 %collective-permute-start = (bf16[3,5120]{1,0:T(4,128)(2,1)S(1)}, bf16[3,5120]{1,0:T(4,128)(2,1)S(1)}, u32[]{:S(2)}, u32[]{:S(2)}) collective-permute-start(bf16[3,5120]{1,0:T(4,128)(2,1)S(1)} %slice_bitcast_fusion.3), channel_id=1, source_target_pairs={{0,1},{1,2},{2,3},{3,4},{4,5},{5,6},{6,7},{7,8},{8,9},{9,10},{10,1... | collective-permute-start | bytes 92168 | tf_op jit(solution)/shard_map/ppermute | solution.py:25
  17.4 1.5 copy-start.6
  20.4 168.3 %copy-start = (f32[8,128,2,128]{3,2,1,0:T(2,128)}, f32[8,128,2,128]{3,2,1,0:T(2,128)S(1)}, u32[]{:S(2)}) copy-start(f32[8,128,2,128]{3,2,1,0:T(2,128)S(1)} %copy.83) | copy-start | bytes 3145732
  182.3 1.9 copy-start.8
  186.3 2.3 copy-start.3
  191.1 3.7 copy-start.9
  193.9 0.8 copy-start.2
  193.9 3.6 copy-start.5
  197.5 243.3 %all-to-all-start = ((bf16[1024,16,128]{2,0,1:T(8,128)(2,1)}), bf16[1024,16,128]{2,0,1:T(8,128)(2,1)}, u32[]{:S(2)}, u32[]{:S(2)}) async-start(bf16[1024,16,128]{2,0,1:T(8,128)(2,1)} %tile.9), calls=%async_computation | async-start | bytes 8388608 | tf_op jit(solution)/shard_map/all_to_all | solution.py:17
  211.9 374.7 %all-gather.7.cloned.1.call-start = ((), (), s32[]{:S(2)}) async-start(), calls=%async_computation.2 | async-start | bytes 8912896 | tf_op jit(solution)/shard_map/all_gather | solution.py:30
  212.9 1.9 copy-start.1
  214.2 2.7 copy-start.4
  615.8 7.2 %copy-start.10 = (f32[1,1024]{1,0:T(1,128)S(1)}, f32[1,1024]{1,0:T(1,128)}, u32[]{:S(2)}) copy-start(f32[1,1024]{1,0:T(1,128)} %param.16) | copy-start | bytes 12292
  628.2 12.6 %collective-permute-start.1 = (bf16[1,128,2048]{2,1,0:T(8,128)(2,1)S(1)}, bf16[1,128,2048]{2,1,0:T(8,128)(2,1)S(1)}, u32[]{:S(2)}, u32[]{:S(2)}) collective-permute-start(bf16[1,128,2048]{2,1,0:T(8,128)(2,1)S(1)} %fusion.27), channel_id=1, source_target_pairs={{0,16},{16,32},{32,48},{48,64},{64,80},{80,96},{96,112},{112,128},... | collective-permute-start | bytes 1572872 | tf_op jit(solution)/shard_map/ppermute | solution.py:45
Sparse Core Ops, SparseCore 0:
  194.9 285.1 all-gather.4
  482.1 104.4 all-gather.6
